TPU v7x, 32 devices: a whole 2x2x4 slice. The times are simulated.
32 devices in a mesh: src: 4 (over y, core), dst: 8 (over z, x).
Axes of the slice: x: 2, y: 2, z: 4, core: 2. Of those that a mesh axis runs over, the one named last changes fastest.
Arguments:
- features: bfloat16 [8192, 768], P(('src', 'dst')), may hold values from -6 to 6
- edge_tiles: bfloat16 [4, 8, 64, 128, 128], P('src', 'dst'), may hold values from -0.3125 to 0.3125
- tile_src: int32 [4, 8, 64], P('src', 'dst'), may hold values from 0 to 7
- tile_dst: int32 [4, 8, 64], P('src', 'dst'), may hold values from 0 to 15, as said below
- tile_count: int32 [4, 8], P('src', 'dst'), may hold values from 1 to 64, as said below
- weight: bfloat16 [768, 1024], replicated, may hold values from -0.21875 to 0.21875
- out_bias: float32 [1024], replicated, may hold values from -3 to 3
- out_grad: bfloat16 [8192, 1024], P(('src', 'dst')), may hold values from -6 to 6
Outputs:
- hidden: bfloat16 [8192, 1024], P(('src', 'dst'))
- feature_grad: bfloat16 [8192, 768], P(('src', 'dst'))
- weight_grad: float32 [768, 1024], replicated
- bias_grad: float32 [1024], replicated
Inputs may be any that keep to these rules, and one draw needn't show every extreme that they name: `tile_src`: block s of the source column of device (i, k) is block s % 2 of device (s // 2, k). `tile_dst`: block e of the destination row of device (i, k) is block e % 2 of device (i, e // 2). On one device, all tile slots whose destination blocks lie on one device name the same block. In every row of devices, slot 0 of every device names one common block. `tile_count`: some device uses all 64 slots.
All inputs are finite; a program needn't handle non-finite values.
Results may differ from a plain program's by a relative error of at most 0.024.
Values may be sent and summed in bfloat16 or wider, within the bound.
A program may use at most 128 MiB of HBM per device.

v0:
```python
import jax
import jax.numpy as jnp
from jax import lax
from jax.sharding import PartitionSpec as P


def per_device(features, edge_tiles, tile_src, tile_dst, tile_count, weight, out_bias, out_grad):
    capacity = edge_tiles.shape[2]
    edge_size = edge_tiles.shape[3]
    feat_width = features.shape[1]
    block_rows = features.shape[0]
    blocks = block_rows // edge_size
    masters = lax.axis_size("dst")
    holders = lax.axis_size("src")
    adjacency = edge_tiles.reshape(capacity, edge_size, edge_size)
    src_ids = tile_src.reshape(capacity)
    dst_ids = tile_dst.reshape(capacity)
    tile_total = tile_count.reshape(())
    alive_mask = jnp.arange(capacity, dtype=jnp.int32) < tile_total
    block_ids = jnp.arange(blocks, dtype=jnp.int32)
    owner_ids = dst_ids // blocks
    inner_ids = dst_ids % blocks
    column = lax.all_gather(features, "src", axis=0, tiled=True).reshape(
        holders * blocks, edge_size, feat_width
    )
    picked = column[src_ids]
    partial_value = jnp.einsum(
        "tij,tjf->tif", adjacency, picked, preferred_element_type=jnp.float32
    )
    routing = (owner_ids[None, :] == jnp.arange(masters, dtype=jnp.int32)[:, None]) & alive_mask[
        None, :
    ]
    outgoing = jnp.einsum("pt,tif->pif", routing.astype(jnp.float32), partial_value)
    wanted_block = jnp.max(jnp.where(routing, inner_ids[None, :], 0), axis=1)
    wanted_rows = jnp.broadcast_to(wanted_block[:, None], (masters, edge_size))
    incoming = lax.all_to_all(
        outgoing.astype(jnp.bfloat16), "dst", split_axis=0, concat_axis=0, tiled=True
    )
    asked = lax.all_to_all(wanted_rows, "dst", split_axis=0, concat_axis=0, tiled=True)
    chooser = (asked[None, :, :] == block_ids[:, None, None]).astype(jnp.bfloat16)
    aggregate = jnp.einsum(
        "jpr,prf->jrf", chooser, incoming, preferred_element_type=jnp.float32
    ).astype(jnp.bfloat16)
    preact = (
        jnp.einsum("jrf,fh->jrh", aggregate, weight, preferred_element_type=jnp.float32) + out_bias
    )
    aggregate, preact, asked = (aggregate, preact, asked)
    gate_value = jax.nn.sigmoid(preact)
    hidden = (preact * gate_value).astype(jnp.bfloat16).reshape(block_rows, -1)
    grad_in = out_grad.reshape(blocks, edge_size, -1).astype(jnp.float32)
    pre_grad = grad_in * (gate_value * (1.0 + preact * (1.0 - gate_value)))
    pre_grad_b = pre_grad.astype(jnp.bfloat16)
    weight_term = jnp.einsum(
        "jrf,jrh->fh", aggregate, pre_grad_b, preferred_element_type=jnp.float32
    )
    bias_term = jnp.sum(pre_grad, axis=(0, 1))
    weight_grad, bias_grad = lax.psum((weight_term, bias_term), ("src", "dst"))
    back = jnp.einsum("jrh,fh->jrf", pre_grad_b, weight, preferred_element_type=jnp.float32).astype(
        jnp.bfloat16
    )
    asked_block = asked[:, 0]
    selector = (asked_block[:, None] == block_ids[None, :]).astype(jnp.bfloat16)
    replies = jnp.einsum("pj,jrf->prf", selector, back, preferred_element_type=jnp.float32).astype(
        jnp.bfloat16
    )
    returned = lax.all_to_all(replies, "dst", split_axis=0, concat_axis=0, tiled=True)
    wanted = returned[owner_ids]
    source = jnp.einsum("tji,tjf->tif", adjacency, wanted, preferred_element_type=jnp.float32)
    src_routing = (
        src_ids[None, :] == jnp.arange(holders * blocks, dtype=jnp.int32)[:, None]
    ) & alive_mask[None, :]
    src_terms = jnp.einsum("kt,tif->kif", src_routing.astype(jnp.float32), source)
    summed = lax.psum_scatter(
        src_terms.reshape(holders * block_rows, feat_width).astype(jnp.bfloat16),
        "src",
        scatter_dimension=0,
        tiled=True,
    )
    return (hidden, summed, weight_grad, bias_grad)


def solution(mesh):
    in_specs = (
        P(("src", "dst"), None),
        P("src", "dst", None, None, None),
        P("src", "dst", None),
        P("src", "dst", None),
        P("src", "dst"),
        P(),
        P(),
        P(("src", "dst"), None),
    )
    out_specs = (P(("src", "dst"), None), P(("src", "dst"), None), P(), P())
    return jax.shard_map(
        per_device, mesh=mesh, in_specs=in_specs, out_specs=out_specs, check_vma=False
    )
```

profile of v0, /device:TPU:0, one launch (start us, length us, event | category | flops | bytes accessed | tf_op | source)
XLA Modules:
  0.0 330.2 jit_solution(10724298226550727925)
XLA Ops:
  7.2 0.0 copy-start
  7.2 0.0 all-gather.2.cloned.1.call-start
  7.2 0.7 all-gather.2.cloned.1.call-update
  8.6 0.7 and_select_fusion.1
  9.2 0.1 select_reduce_fusion
  9.4 0.7 broadcast_in_dim.16
  10.0 7.3 %all-to-all-start.1 = ((s32[8,1,128]{2,1,0:T(1,128)}), s32[8,1,128]{2,1,0:T(1,128)S(1)}, u32[]{:S(2)}, u32[]{:S(2)}) async-start(s32[8,1,128]{2,1,0:T(1,128)} %broadcast_in_dim.16), calls=%async_computation.1 | async-start | bytes 8192 | tf_op jit(solution)/shard_map/all_to_all | solution.py:39
  17.3 0.7 fusion.39
  18.0 14.0 %all-gather.2.cloned.1.call-done = bf16[1024,768]{1,0:T(8,128)(2,1)} async-done(((bf16[256,768]{1,0:T(8,128)(2,1)}), bf16[1024,768]{1,0:T(8,128)(2,1)}) %all-gather.2.cloned.1.call-update) | async-done | bytes 1572880 | tf_op jit(solution)/shard_map/all_gather | solution.py:23
  31.9 8.7 %gather_fusion = bf16[64,128,768]{2,1,0:T(8,128)(2,1)} fusion(bf16[8,128,768]{2,1,0:T(8,128)(2,1)} %bitcast.81, s32[1024]{0:T(1024)S(1)} %pad_clamp_fusion.1), kind=kCustom, calls=%fused_computation | custom fusion | bytes 25166080 | tf_op jit(solution)/shard_map/gather | solution.py:26
  40.6 0.0 copy-done
  40.6 9.1 %convolution_bitcast_fusion.1 = bf16[64,128,768]{1,2,0:T(8,128)(2,1)} fusion(bf16[64,128,768]{2,1,0:T(8,128)(2,1)} %gather_fusion, bf16[1,1,64,128,128]{4,3,2,1,0:T(8,128)(2,1)S(1)} %copy-done), kind=kOutput, calls=%fused_computation.3 | convolution fusion | flops 1610612736 | bytes 27262976 | tf_op jit(solution)/shard_map/tij,tjf->tif/dot_general | solution.py:27
  49.7 16.8 %copy.40 = bf16[64,128,768]{2,0,1:T(8,128)(2,1)} copy(bf16[64,128,768]{1,2,0:T(8,128)(2,1)} %convolution_bitcast_fusion.1) | data formatting | bytes 25165824 | tf_op jit(solution)/shard_map/tij,tjf->tif/dot_general | solution.py:27
  66.5 6.3 %convolution_convert_fusion.2 = bf16[8,128,768]{2,0,1:T(8,128)(2,1)S(1)} fusion(bf16[64,128,768]{2,0,1:T(8,128)(2,1)} %copy.40, s32[64]{0:T(128)S(1)} %get-tuple-element.8, pred[64]{0:T(512)(128)(4,1)S(1)} %iota_compare_fusion.2), kind=kOutput, calls=%fused_computation.9 | convolution fusion | flops 100664320 | bytes 14156096 | tf_op jit(solution)/shard_map/pt,tif->pif/dot_general | solution.py:33
  72.8 1.5 copy.41
  74.3 0.0 all-to-all-done.1
  74.3 5.5 %all-to-all-start = ((bf16[8,128,768]{2,1,0:T(8,128)(2,1)}), bf16[8,128,768]{2,1,0:T(8,128)(2,1)}, u32[]{:S(2)}, u32[]{:S(2)}) async-start(bf16[8,128,768]{2,1,0:T(8,128)(2,1)} %copy.41), calls=%async_computation | async-start | bytes 3145728 | tf_op jit(solution)/shard_map/all_to_all | solution.py:36
  79.8 0.0 copy-start.4
  79.8 0.1 copy.42
  79.9 0.1 slice_reduce_fusion
  80.0 37.2 %all-to-all-done = bf16[8,128,768]{2,1,0:T(8,128)(2,1)} async-done(((bf16[8,128,768]{2,1,0:T(8,128)(2,1)}), bf16[8,128,768]{2,1,0:T(8,128)(2,1)}, u32[]{:S(2)}, u32[]{:S(2)}) %all-to-all-start) | async-done | bytes 1572896 | tf_op jit(solution)/shard_map/all_to_all | solution.py:36
  117.3 2.6 fusion.17
  119.8 0.5 copy.50
  120.3 0.0 copy-done.3
  120.3 0.0 copy-done.4
  120.3 0.0 copy-start.2
  120.3 3.3 %fusion.42 = (f32[1024]{0:T(1024)S(1)}, bf16[2,128,1024]{2,1,0:T(8,128)(2,1)S(1)}, bf16[2,128,1024]{2,1,0:T(8,128)(2,1)}) fusion(bf16[2,128,1024]{2,1,0:T(8,128)(2,1)S(1)} %bitcast.86, f32[1024]{0:T(1024)S(1)} %copy-done.4, bf16[2,128,768]{1,2,0:T(8,128)(2,1)S(1)} %copy.50, bf16[768,1024]{1,0:T(8,128)(2,1)} %param.13), kind=kOutput, calls=%fused_computation.63 | convolution fusion | flops 406322176 | bytes 3547136 | tf_op jit(solution)/shard_map/jrf,fh->jrh/dot_general | solution.py:45
  123.7 0.0 copy-done.2
  123.7 0.7 fusion.14
  124.3 0.7 convolution_convert_fusion.1
  125.0 1.4 copy.46
  126.5 4.4 %all-to-all-start.2 = ((bf16[8,128,768]{2,1,0:T(8,128)(2,1)}), bf16[8,128,768]{2,1,0:T(8,128)(2,1)}, u32[]{:S(2)}, u32[]{:S(2)}) async-start(bf16[8,128,768]{2,1,0:T(8,128)(2,1)} %copy.46), calls=%async_computation.2 | async-start | bytes 3145728 | tf_op jit(solution)/shard_map/all_to_all | solution.py:66
  130.9 0.0 all-reduce.2.cloned.1.call-start
  131.0 2.2 convolution_bitcast_fusion.2
  133.2 0.0 all-reduce.2.cloned.1.call-update
  133.3 0.2 reduce-scatter.2.cloned.1.call-start
  133.5 44.2 %all-to-all-done.2 = bf16[8,128,768]{2,1,0:T(8,128)(2,1)} async-done(((bf16[8,128,768]{2,1,0:T(8,128)(2,1)}), bf16[8,128,768]{2,1,0:T(8,128)(2,1)}, u32[]{:S(2)}, u32[]{:S(2)}) %all-to-all-start.2) | async-done | bytes 1572896 | tf_op jit(solution)/shard_map/all_to_all | solution.py:66
  177.7 8.7 %gather_fusion.1 = bf16[64,128,768]{2,1,0:T(8,128)(2,1)} fusion(bf16[8,128,768]{2,1,0:T(8,128)(2,1)} %all-to-all-done.2, s32[1024]{0:T(1024)S(1)} %pad_clamp_fusion), kind=kCustom, calls=%fused_computation.1 | custom fusion | bytes 25166080 | tf_op jit(solution)/shard_map/gather | solution.py:67
  186.4 9.3 %convolution_bitcast_fusion = bf16[64,128,768]{1,2,0:T(8,128)(2,1)} fusion(bf16[64,128,768]{2,1,0:T(8,128)(2,1)} %gather_fusion.1, bf16[1,1,64,128,128]{4,3,2,1,0:T(8,128)(2,1)S(1)} %copy-done), kind=kOutput, calls=%fused_computation.2 | convolution fusion | flops 1610612736 | bytes 27262976 | tf_op jit(solution)/shard_map/tji,tjf->tif/dot_general | solution.py:68
  195.7 16.8 %copy.48 = bf16[64,128,768]{2,0,1:T(8,128)(2,1)} copy(bf16[64,128,768]{1,2,0:T(8,128)(2,1)} %convolution_bitcast_fusion) | data formatting | bytes 25165824 | tf_op jit(solution)/shard_map/tji,tjf->tif/dot_general | solution.py:68
  212.5 0.0 copy-done.1
  212.5 6.3 %convolution_convert_fusion = bf16[8,128,768]{2,0,1:T(8,128)(2,1)S(1)} fusion(bf16[64,128,768]{2,0,1:T(8,128)(2,1)} %copy.48, s32[64]{0:T(128)S(1)} %bitcast.85, pred[64]{0:T(512)(128)(4,1)S(1)} %iota_compare_fusion.2), kind=kOutput, calls=%fused_computation.7 | convolution fusion | flops 100664320 | bytes 14156096 | tf_op jit(solution)/shard_map/kt,tif->kif/dot_general | solution.py:72
  218.9 1.5 copy.49
  220.3 0.0 reduce-scatter.2.cloned.1.call-update
  220.4 38.4 %psum.15 = f32[1024]{0:T(1024)} all-reduce(f32[1024]{0:T(1024)S(1)} %get-tuple-element.4), channel_id=1, replica_groups=mesh['src'=4,'dst'=8] {'src','dst'}, use_global_device_ids=true, to_apply=%region_4.5 | all-reduce | flops 1024 | bytes 8192 | tf_op jit(solution)/shard_map/psum | solution.py:57
  258.8 31.0 %all-reduce.2.cloned.1.call-done = f32[768,1024]{1,0:T(8,128)} async-done(((f32[768,1024]{1,0:T(8,128)}), f32[768,1024]{1,0:T(8,128)}) %all-reduce.2.cloned.1.call-update) | async-done | bytes 3145744 | tf_op jit(solution)/shard_map/psum | solution.py:57
  289.8 29.9 %reduce-scatter.2.cloned.1.call-done = bf16[256,768]{1,0:T(8,128)(2,1)} async-done(((bf16[1024,768]{1,0:T(8,128)(2,1)}), bf16[256,768]{1,0:T(8,128)(2,1)}) %reduce-scatter.2.cloned.1.call-update) | async-done | bytes 393232 | tf_op jit(solution)/shard_map/reduce_scatter | solution.py:73
  319.7 4.0 %copy.63 = f32[768,1024]{1,0:T(8,128)} copy(f32[768,1024]{1,0:T(8,128)} %all-reduce.2.cloned.1.call-done) | data formatting | bytes 6291456
  (8 shorter events, 0.0 us)
Async XLA Ops:
  7.2 33.4 %copy-start = (bf16[1,1,64,128,128]{4,3,2,1,0:T(8,128)(2,1)S(1)}, bf16[1,1,64,128,128]{4,3,2,1,0:T(8,128)(2,1)}, u32[]{:S(2)}) copy-start(bf16[1,1,64,128,128]{4,3,2,1,0:T(8,128)(2,1)} %param.9) | copy-start | bytes 6291460
  7.2 24.8 %all-gather.2.cloned.1.call-start = ((), (), s32[]{:S(2)}) async-start(), calls=%async_computation.4 | async-start | bytes 1966080 | tf_op jit(solution)/shard_map/all_gather | solution.py:23
  10.0 64.2 %all-to-all-start.1 = ((s32[8,1,128]{2,1,0:T(1,128)}), s32[8,1,128]{2,1,0:T(1,128)S(1)}, u32[]{:S(2)}, u32[]{:S(2)}) async-start(s32[8,1,128]{2,1,0:T(1,128)} %broadcast_in_dim.16), calls=%async_computation.1 | async-start | bytes 8192 | tf_op jit(solution)/shard_map/all_to_all | solution.py:39
  74.3 43.0 %all-to-all-start = ((bf16[8,128,768]{2,1,0:T(8,128)(2,1)}), bf16[8,128,768]{2,1,0:T(8,128)(2,1)}, u32[]{:S(2)}, u32[]{:S(2)}) async-start(bf16[8,128,768]{2,1,0:T(8,128)(2,1)} %copy.41), calls=%async_computation | async-start | bytes 3145728 | tf_op jit(solution)/shard_map/all_to_all | solution.py:36
  79.8 40.5 %copy-start.3 = (bf16[256,1024]{1,0:T(8,128)(2,1)S(1)}, bf16[256,1024]{1,0:T(8,128)(2,1)}, u32[]{:S(2)}) copy-start(bf16[256,1024]{1,0:T(8,128)(2,1)} %param.15) | copy-start | bytes 1572868
  79.8 40.5 %copy-start.4 = (f32[1024]{0:T(1024)S(1)}, f32[1024]{0:T(1024)}, u32[]{:S(2)}) copy-start(f32[1024]{0:T(1024)} %param.14) | copy-start | bytes 12292
  120.3 3.3 %copy-start.2 = (bf16[768,1024]{1,0:T(8,128)(2,1)S(1)}, bf16[768,1024]{1,0:T(8,128)(2,1)}, u32[]{:S(2)}) copy-start(bf16[768,1024]{1,0:T(8,128)(2,1)} %param.13) | copy-start | bytes 4718596
  126.5 4.5 %copy-start.5 = (s32[1,1,64]{2,1,0:T(1,128)S(1)}, s32[1,1,64]{2,1,0:T(1,128)}, u32[]{:S(2)}) copy-start(s32[1,1,64]{2,1,0:T(1,128)} %param.11) | copy-start | bytes 772
  126.5 51.2 %all-to-all-start.2 = ((bf16[8,128,768]{2,1,0:T(8,128)(2,1)}), bf16[8,128,768]{2,1,0:T(8,128)(2,1)}, u32[]{:S(2)}, u32[]{:S(2)}) async-start(bf16[8,128,768]{2,1,0:T(8,128)(2,1)} %copy.46), calls=%async_computation.2 | async-start | bytes 3145728 | tf_op jit(solution)/shard_map/all_to_all | solution.py:66
  130.9 158.9 %all-reduce.2.cloned.1.call-start = ((), (), s32[]{:S(2)}) async-start(), calls=%async_computation.6 | async-start | bytes 6291456 | tf_op jit(solution)/shard_map/psum | solution.py:57
  133.3 186.4 %reduce-scatter.2.cloned.1.call-start = ((), (), s32[]{:S(2)}) async-start(), calls=%async_computation.5 | async-start | bytes 1966080 | tf_op jit(solution)/shard_map/reduce_scatter | solution.py:73
  195.7 16.8 %copy-start.1 = (s32[1,1,64]{2,1,0:T(1,128)S(1)}, s32[1,1,64]{2,1,0:T(1,128)}, u32[]{:S(2)}) copy-start(s32[1,1,64]{2,1,0:T(1,128)} %param.10) | copy-start | bytes 772
Sparse Core Ops, SparseCore 0:
  9.5 22.3 all-gather.1
  137.8 151.9 all-reduce.1
  292.9 26.7 reduce-scatter.1
where the time goes:
time: 331 us; the launch traced here: 330 us
  waiting for transfers between devices  157 us (47%)
  local copies, waits for them, and re-layouts  60.7 us (18%)
  matrix products  40.5 us (12%)
  blocking collectives  38.4 us (12%)
  starting transfers between devices  17.5 us (5%)
  between operations  14.5 us (4%)
    all_to_all x1, waiting for transfers between devices, per_device(): lax.all_to_all(replies, 'dst', split_axis=0, concat_axis=0, tiled=True)  44.2 us
    psum x1, blocking collectives, per_device(): weight_grad, bias_grad = lax.psum((weight_term, bias_term), ('src', 'dst'))  38.4 us
    all_to_all x1, waiting for transfers between devices, per_device(): lax.all_to_all(outgoing.astype(jnp.bfloat16), 'dst', split_axis=0, concat...  37.2 us
    psum x1, waiting for transfers between devices, per_device(): weight_grad, bias_grad = lax.psum((weight_term, bias_term), ('src', 'dst'))  31 us
    reduce_scatter x1, waiting for transfers between devices, per_device(): lax.psum_scatter(src_terms.reshape(holders * block_rows, feat_width).asty...  29.9 us
    dot_general x1, local copies, waits for them, and re-layouts, per_device(): jnp.einsum('tji,tjf->tif', adjacency, wanted, preferred_element_type=jnp....  16.8 us
    dot_general x1, local copies, waits for them, and re-layouts, per_device(): jnp.einsum('tij,tjf->tif', adjacency, picked, preferred_element_type=jnp....  16.8 us
    all_gather x1, waiting for transfers between devices, per_device(): lax.all_gather(features, 'src', axis=0, tiled=True)  14 us
  transfers between devices with their start and end apart: 6, of which 5 were waited for; matrix products, arithmetic and copies ran while one was open for 27% of the time, Pallas kernels for 0%

commit v1 on v0

v1 whole, which is shorter than its diff:
```python
import jax
import jax.numpy as jnp
from jax import lax
from jax.experimental import pallas as pl
from jax.experimental.pallas import tpu as pltpu
from jax.sharding import PartitionSpec as P


def block_matrix_kernel(blocks, src_ref, dst_ref, count_ref, tiles_ref, out_ref, total):
    size = tiles_ref.shape[1]
    total[...] = jnp.zeros_like(total)

    def add_tile(slot, carry):
        row = pl.multiple_of(dst_ref[slot] // blocks * size, size)
        col = pl.multiple_of(src_ref[slot] * size, size)
        total[pl.ds(row, size), pl.ds(col, size)] += tiles_ref[slot].astype(jnp.float32)
        return carry

    lax.fori_loop(0, count_ref[0], add_tile, 0)
    out_ref[...] = total[...].astype(out_ref.dtype)


def block_matrix(src_ids, dst_ids, tile_total, tiles, blocks, masters, columns):
    size = tiles.shape[1]
    shape = (masters * size, columns * size)
    smem = pl.BlockSpec(memory_space=pltpu.SMEM)
    vmem = pl.BlockSpec(memory_space=pltpu.VMEM)
    held = tiles.size * 2 + shape[0] * shape[1] * 6
    return pl.pallas_call(
        lambda *refs: block_matrix_kernel(blocks, *refs),
        out_shape=jax.ShapeDtypeStruct(shape, jnp.bfloat16),
        in_specs=[smem, smem, smem, vmem],
        out_specs=vmem,
        scratch_shapes=[pltpu.VMEM(shape, jnp.float32)],
        compiler_params=pltpu.CompilerParams(vmem_limit_bytes=held + 4 * 1024 * 1024),
        cost_estimate=pl.CostEstimate(flops=tiles.size, bytes_accessed=held, transcendentals=0),
        name="block_matrix",
    )(src_ids, dst_ids, tile_total, tiles)


def scatter_sum(terms):
    chips = terms.shape[0]
    holders = chips * 2
    me = lax.axis_index("src")
    core = me % 2
    chip = me // 2
    kept = jnp.where(core == 0, terms[:, 0], terms[:, 1])
    given = jnp.where(core == 0, terms[:, 1], terms[:, 0]).astype(jnp.bfloat16)
    got = lax.ppermute(given, "src", [(i, i ^ 1) for i in range(holders)])
    pair = kept + got.astype(jnp.float32)
    result = lax.dynamic_index_in_dim(pair, chip, 0, keepdims=False)
    sent = pair.astype(jnp.bfloat16)
    for step in range(1, chips):
        out = lax.dynamic_index_in_dim(sent, (chip + step) % chips, 0, keepdims=False)
        ring = [(i, (i + 2 * step) % holders) for i in range(holders)]
        result = result + lax.ppermute(out, "src", ring).astype(jnp.float32)
    return result.astype(jnp.bfloat16)


def per_device(features, edge_tiles, tile_src, tile_dst, tile_count, weight, out_bias, out_grad):
    capacity = edge_tiles.shape[2]
    edge_size = edge_tiles.shape[3]
    feat_width = features.shape[1]
    block_rows = features.shape[0]
    blocks = block_rows // edge_size
    masters = lax.axis_size("dst")
    holders = lax.axis_size("src")
    adjacency = edge_tiles.reshape(capacity, edge_size, edge_size)
    src_ids = tile_src.reshape(capacity)
    dst_ids = tile_dst.reshape(capacity)
    tile_total = tile_count.reshape(())
    alive_mask = jnp.arange(capacity, dtype=jnp.int32) < tile_total
    block_ids = jnp.arange(blocks, dtype=jnp.int32)
    owner_ids = dst_ids // blocks
    inner_ids = dst_ids % blocks
    column = lax.all_gather(features, "src", axis=0, tiled=True)
    matrix = block_matrix(
        src_ids, dst_ids, tile_count.reshape(1), adjacency, blocks, masters, holders * blocks
    )
    routing = (owner_ids[None, :] == jnp.arange(masters, dtype=jnp.int32)[:, None]) & alive_mask[
        None, :
    ]
    wanted_block = jnp.max(jnp.where(routing, inner_ids[None, :], 0), axis=1)
    wanted_rows = jnp.broadcast_to(wanted_block[:, None], (masters, edge_size))
    asked = lax.all_to_all(wanted_rows, "dst", split_axis=0, concat_axis=0, tiled=True)
    outgoing = jnp.dot(matrix, column, preferred_element_type=jnp.float32).astype(jnp.bfloat16)
    incoming = lax.all_to_all(
        outgoing.reshape(masters, edge_size, feat_width),
        "dst",
        split_axis=0,
        concat_axis=0,
        tiled=True,
    )
    asked_block = asked[:, 0]
    selector = asked_block[:, None] == block_ids[None, :]
    aggregate = jnp.concatenate(
        [
            jnp.sum(
                jnp.where(selector[:, j, None, None], incoming.astype(jnp.float32), 0.0), axis=0
            ).astype(jnp.bfloat16)
            for j in range(blocks)
        ],
        axis=0,
    )
    preact = jnp.dot(aggregate, weight, preferred_element_type=jnp.float32) + out_bias
    gate_value = jax.nn.sigmoid(preact)
    hidden = (preact * gate_value).astype(jnp.bfloat16)
    pre_grad = out_grad.astype(jnp.float32) * (gate_value * (1.0 + preact * (1.0 - gate_value)))
    pre_grad_b = pre_grad.astype(jnp.bfloat16)
    weight_term = lax.dot_general(
        aggregate, pre_grad_b, (((0,), (0,)), ((), ())), preferred_element_type=jnp.float32
    )
    bias_term = jnp.sum(pre_grad, axis=0, keepdims=True)
    joined = jnp.concatenate(
        [weight_term.astype(jnp.bfloat16), jnp.broadcast_to(bias_term, (16, bias_term.shape[1])).astype(jnp.bfloat16)],
        axis=0,
    )
    reduced = lax.psum(joined, ("src", "dst"))
    weight_grad = reduced[:feat_width].astype(jnp.float32)
    bias_grad = reduced[feat_width].astype(jnp.float32)
    back = lax.dot_general(
        pre_grad_b, weight, (((1,), (1,)), ((), ())), preferred_element_type=jnp.float32
    ).astype(jnp.bfloat16)
    back = back.reshape(blocks, edge_size, feat_width)
    replies = back[0][None]
    for j in range(1, blocks):
        replies = jnp.where(selector[:, j, None, None], back[j][None], replies)
    returned = lax.all_to_all(replies, "dst", split_axis=0, concat_axis=0, tiled=True)
    src_terms = lax.dot_general(
        matrix,
        returned.reshape(masters * edge_size, feat_width),
        (((0,), (0,)), ((), ())),
        preferred_element_type=jnp.float32,
    )
    summed = scatter_sum(src_terms.reshape(holders // 2, 2, block_rows, feat_width))
    return (hidden, summed, weight_grad, bias_grad)


def solution(mesh):
    in_specs = (
        P(("src", "dst"), None),
        P("src", "dst", None, None, None),
        P("src", "dst", None),
        P("src", "dst", None),
        P("src", "dst"),
        P(),
        P(),
        P(("src", "dst"), None),
    )
    out_specs = (P(("src", "dst"), None), P(("src", "dst"), None), P(), P())
    return jax.shard_map(
        per_device, mesh=mesh, in_specs=in_specs, out_specs=out_specs, check_vma=False
    )
```

time: 331 us -> 277 us (0.84)
  waiting for transfers between devices: 157 us -> 207 us
  local copies, waits for them, and re-layouts: 60.7 us -> 12.3 us
  blocking collectives: 38.4 us -> 0 us
  matrix products: 40.5 us -> 11.3 us
  other arithmetic: 1.48 us -> 12.2 us
    psum x1, waiting for transfers between devices: 31 us -> 127 us  [per_device(): reduced = lax.psum(joined, ('src', 'dst'))]
    psum x1 -> x0, blocking collectives: 38.4 us -> none  [per_device(): weight_grad, bias_grad = lax.psum((weight_term, bias_term), ('src', 'dst'))]
    reduce_scatter x1 -> x0, waiting for transfers between devices: 29.9 us -> none  [per_device(): lax.psum_scatter(src_terms.reshape(holders * block_rows, feat_width).asty...]
    dot_general x2 -> x1, local copies, waits for them, and re-layouts: 33.6 us -> 3.94 us  [per_device(): lax.dot_general(matrix, returned.reshape(masters * edge_size, feat_width)...]
    dot_general x9 -> x5, matrix products: 40.5 us -> 11.3 us  [the longest x1 4.98 us: per_device(): jnp.dot(matrix, column, preferred_element_type=jnp.float32)]
    gather x2 -> x0, local copies, waits for them, and re-layouts: 17.3 us -> none  [the longest x1 8.68 us: per_device(): wanted = returned[owner_ids]]
    all_to_all x1, waiting for transfers between devices: 44.2 us -> 33.2 us  [per_device(): lax.all_to_all(replies, 'dst', split_axis=0, concat_axis=0, tiled=True)]
    convert_element_type x0 -> x4, other arithmetic: none -> 5.73 us  [the longest x1 3.46 us: per_device(): weight_grad = reduced[:feat_width].astype(jnp.float32)]
  transfers between devices with their start and end apart: 6 -> 7, of which waited for: 5 -> 4; matrix products, arithmetic and copies ran while one was open for 27% -> 7% of each run, Pallas kernels for 0% -> 0%
where the time goes in v1:
time: 277 us; the launch traced here: 276 us
  waiting for transfers between devices  207 us (75%)
  starting transfers between devices  17.1 us (6%)
  between operations  14.9 us (5%)
  local copies, waits for them, and re-layouts  12.3 us (4%)
  other arithmetic  12.2 us (4%)
  matrix products  11.3 us (4%)
    psum x1, waiting for transfers between devices, per_device(): reduced = lax.psum(joined, ('src', 'dst'))  127 us
    all_to_all x1, waiting for transfers between devices, per_device(): lax.all_to_all(outgoing.reshape(masters, edge_size, feat_width), 'dst', s...  37.3 us
    all_to_all x1, waiting for transfers between devices, per_device(): lax.all_to_all(replies, 'dst', split_axis=0, concat_axis=0, tiled=True)  33.2 us
    all_gather x1, waiting for transfers between devices, per_device(): column = lax.all_gather(features, 'src', axis=0, tiled=True)  9.05 us
    all_to_all x1, starting transfers between devices, per_device(): lax.all_to_all(wanted_rows, 'dst', split_axis=0, concat_axis=0, tiled=True)  7.28 us
    unnamed x20, local copies, waits for them, and re-layouts  6.72 us
  transfers between devices with their start and end apart: 7, of which 4 were waited for; matrix products, arithmetic and copies ran while one was open for 7% of the time, Pallas kernels for 0%

profile of v1, /device:TPU:0, one launch (start us, length us, event | category | flops | bytes accessed | tf_op | source)
XLA Modules:
  0.0 276.0 jit_solution(6293729831422772492)
XLA Ops:
  7.2 0.0 copy-start
  7.2 0.0 all-gather.2.cloned.1.call-start
  7.2 0.7 all-gather.2.cloned.1.call-update
  8.6 0.7 and_select_fusion.1
  9.2 0.1 select_reduce_fusion
  9.4 0.7 broadcast_in_dim.76
  10.0 7.3 %all-to-all-start = ((s32[8,1,128]{2,1,0:T(1,128)}), s32[8,1,128]{2,1,0:T(1,128)S(1)}, u32[]{:S(2)}, u32[]{:S(2)}) async-start(s32[8,1,128]{2,1,0:T(1,128)} %broadcast_in_dim.76), calls=%async_computation | async-start | bytes 8192 | tf_op jit(solution)/shard_map/all_to_all | solution.py:85
  17.3 1.7 copy-done.2
  19.0 0.7 copy-done.3
  19.7 0.7 copy-done.4
  20.3 1.2 block_matrix.1
  21.6 0.0 copy-start.1
  21.6 1.3 copy-done.1
  22.9 9.0 %all-gather.2.cloned.1.call-done = bf16[1024,768]{1,0:T(8,128)(2,1)} async-done(((bf16[256,768]{1,0:T(8,128)(2,1)}), bf16[1024,768]{1,0:T(8,128)(2,1)}) %all-gather.2.cloned.1.call-update) | async-done | bytes 1572880 | tf_op jit(solution)/shard_map/all_gather | solution.py:76
  31.9 5.0 %convolution_convert_fusion.1 = bf16[1024,768]{1,0:T(8,128)(2,1)} fusion(bf16[1024,1024]{1,0:T(8,128)(2,1)} %copy-done.1, bf16[1024,768]{1,0:T(8,128)(2,1)} %all-gather.2.cloned.1.call-done), kind=kOutput, calls=%fused_computation.5 | convolution fusion | flops 1611399168 | bytes 5242880 | tf_op jit(solution)/shard_map/dot_general | solution.py:86
  36.9 0.0 all-to-all-done
  36.9 5.5 %all-to-all-start.1 = ((bf16[8,128,768]{2,1,0:T(8,128)(2,1)}), bf16[8,128,768]{2,1,0:T(8,128)(2,1)S(1)}, u32[]{:S(2)}, u32[]{:S(2)}) async-start(bf16[8,128,768]{2,1,0:T(8,128)(2,1)} %bitcast.67), calls=%async_computation.1 | async-start | bytes 3145728 | tf_op jit(solution)/shard_map/all_to_all | solution.py:87
  42.4 0.1 slice_reduce_fusion
  42.6 37.3 %all-to-all-done.1 = bf16[8,128,768]{2,1,0:T(8,128)(2,1)S(1)} async-done(((bf16[8,128,768]{2,1,0:T(8,128)(2,1)}), bf16[8,128,768]{2,1,0:T(8,128)(2,1)S(1)}, u32[]{:S(2)}, u32[]{:S(2)}) %all-to-all-start.1) | async-done | bytes 1572896 | tf_op jit(solution)/shard_map/all_to_all | solution.py:87
  79.8 0.6 fusion
  80.4 0.0 copy-done
  80.5 0.0 copy-done.9
  80.5 0.4 copy-done.8
  80.9 1.8 fusion.12
  82.6 0.8 copy-done.6
  83.4 0.6 convolution_convert_fusion.2
  84.1 1.4 broadcast_select_fusion
  85.5 3.6 %all-to-all-start.2 = ((bf16[8,128,768]{2,1,0:T(8,128)(2,1)}), bf16[8,128,768]{2,1,0:T(8,128)(2,1)S(1)}, u32[]{:S(2)}, u32[]{:S(2)}) async-start(bf16[8,128,768]{2,1,0:T(8,128)(2,1)} %broadcast_select_fusion), calls=%async_computation.2 | async-start | bytes 3145728 | tf_op jit(solution)/shard_map/all_to_all | solution.py:128
  89.1 0.0 all-reduce.2.cloned.1.call-start
  89.1 3.9 %copy.33 = bf16[1024,1024]{1,0:T(8,128)(2,1)} copy(bf16[1024,1024]{0,1:T(8,128)(2,1)} %bitcast.61) | data formatting | bytes 4194304 | tf_op jit(solution)/shard_map/dot_general | solution.py:129
  93.1 33.2 %all-to-all-done.2 = bf16[8,128,768]{2,1,0:T(8,128)(2,1)S(1)} async-done(((bf16[8,128,768]{2,1,0:T(8,128)(2,1)}), bf16[8,128,768]{2,1,0:T(8,128)(2,1)S(1)}, u32[]{:S(2)}, u32[]{:S(2)}) %all-to-all-start.2) | async-done | bytes 1572896 | tf_op jit(solution)/shard_map/all_to_all | solution.py:128
  126.3 3.4 %fusion.14 = f32[2,2,256,768]{3,2,1,0:T(8,128)S(1)} fusion(bf16[2,2,256,1024]{3,2,1,0:T(8,128)(2,1)} %bitcast.65, bf16[1024,768,1,1]{1,0,3,2:T(8,128)(2,1)S(1)} %bitcast.66), kind=kOutput, calls=%fused_computation.44 | convolution fusion | flops 1610612736 | bytes 6815744 | tf_op jit(solution)/shard_map/dot_general | solution.py:129
  129.7 0.0 copy-start.5
  129.7 0.1 fusion.4
  129.8 0.1 collective-permute-start
  129.9 1.2 copy-done.7
  131.1 0.6 convolution_convert_fusion
  131.7 1.3 pad_maximum_fusion
  133.0 0.0 all-reduce.2.cloned.1.call-update
  133.1 0.0 collective-permute-done
  133.1 2.4 fusion.3
  135.4 0.8 fusion.6
  136.2 0.6 collective-permute-start.1
  136.8 126.7 %all-reduce.2.cloned.1.call-done = bf16[784,1024]{1,0:T(8,128)(2,1)} async-done(((bf16[784,1024]{1,0:T(8,128)(2,1)}), bf16[784,1024]{1,0:T(8,128)(2,1)}) %all-reduce.2.cloned.1.call-update) | async-done | bytes 1605648 | tf_op jit(solution)/shard_map/psum | solution.py:118
  263.5 1.3 slice_convert_fusion.1
  264.8 3.5 %slice_convert_fusion = f32[768,1024]{1,0:T(8,128)} fusion(bf16[784,1024]{1,0:T(8,128)(2,1)} %all-reduce.2.cloned.1.call-done), kind=kLoop, calls=%fused_computation.7 | loop fusion | flops 786432 | bytes 4718592 | tf_op jit(solution)/shard_map/convert_element_type | solution.py:119
  268.3 0.0 collective-permute-done.1
  268.3 0.8 fusion.5
  (13 shorter events, 0.1 us)
Async XLA Ops:
  7.2 73.3 %copy-start = (bf16[768,1024]{1,0:T(8,128)(2,1)S(1)}, bf16[768,1024]{1,0:T(8,128)(2,1)}, u32[]{:S(2)}) copy-start(bf16[768,1024]{1,0:T(8,128)(2,1)} %param.13) | copy-start | bytes 4718596
  7.2 24.8 %all-gather.2.cloned.1.call-start = ((), (), s32[]{:S(2)}) async-start(), calls=%async_computation.3 | async-start | bytes 1966080 | tf_op jit(solution)/shard_map/all_gather | solution.py:76
  10.0 26.9 %all-to-all-start = ((s32[8,1,128]{2,1,0:T(1,128)}), s32[8,1,128]{2,1,0:T(1,128)S(1)}, u32[]{:S(2)}, u32[]{:S(2)}) async-start(s32[8,1,128]{2,1,0:T(1,128)} %broadcast_in_dim.76), calls=%async_computation | async-start | bytes 8192 | tf_op jit(solution)/shard_map/all_to_all | solution.py:85
  17.3 1.7 copy-start.2
  19.0 0.7 copy-start.3
  19.7 0.7 copy-start.4
  21.6 1.3 copy-start.1
  36.9 42.9 %all-to-all-start.1 = ((bf16[8,128,768]{2,1,0:T(8,128)(2,1)}), bf16[8,128,768]{2,1,0:T(8,128)(2,1)S(1)}, u32[]{:S(2)}, u32[]{:S(2)}) async-start(bf16[8,128,768]{2,1,0:T(8,128)(2,1)} %bitcast.67), calls=%async_computation.1 | async-start | bytes 3145728 | tf_op jit(solution)/shard_map/all_to_all | solution.py:87
  42.4 38.0 %copy-start.9 = (f32[1024]{0:T(1024)S(1)}, f32[1024]{0:T(1024)}, u32[]{:S(2)}) copy-start(f32[1024]{0:T(1024)} %param.14) | copy-start | bytes 12292
  79.8 1.0 copy-start.8
  82.6 0.8 copy-start.6
  85.5 40.8 %all-to-all-start.2 = ((bf16[8,128,768]{2,1,0:T(8,128)(2,1)}), bf16[8,128,768]{2,1,0:T(8,128)(2,1)S(1)}, u32[]{:S(2)}, u32[]{:S(2)}) async-start(bf16[8,128,768]{2,1,0:T(8,128)(2,1)} %broadcast_select_fusion), calls=%async_computation.2 | async-start | bytes 3145728 | tf_op jit(solution)/shard_map/all_to_all | solution.py:128
  89.1 174.4 %all-reduce.2.cloned.1.call-start = ((), (), s32[]{:S(2)}) async-start(), calls=%async_computation.4 | async-start | bytes 3211264 | tf_op jit(solution)/shard_map/psum | solution.py:118
  129.7 2.0 copy-start.5
  129.7 1.4 copy-start.7
  129.8 3.2 %collective-permute-start = (bf16[2,256,768]{2,1,0:T(8,128)(2,1)S(1)}, bf16[2,256,768]{2,1,0:T(8,128)(2,1)}, u32[]{:S(2)}, u32[]{:S(2)}) collective-permute-start(bf16[2,256,768]{2,1,0:T(8,128)(2,1)S(1)} %fusion.4), channel_id=1, source_target_pairs={{0,8},{8,0},{16,24},{24,16},{1,9},{9,1},{17,25},{25,17},{2,10},{10... | collective-permute-start | bytes 2359304 | tf_op jit(solution)/shard_map/ppermute | solution.py:49
  136.2 132.1 %collective-permute-start.1 = (bf16[256,768]{1,0:T(8,128)(2,1)}, bf16[256,768]{1,0:T(8,128)(2,1)S(1)}, u32[]{:S(2)}, u32[]{:S(2)}) collective-permute-start(bf16[256,768]{1,0:T(8,128)(2,1)} %fusion.6), channel_id=1, source_target_pairs={{0,16},{8,24},{16,0},{24,8},{1,17},{9,25},{17,1},{25,9},{2,18},{10... | collective-permute-start | bytes 1179656 | tf_op jit(solution)/shard_map/ppermute | solution.py:56
Sparse Core Ops, SparseCore 0:
  9.5 22.3 all-gather.1
  133.1 130.3 all-reduce.1
